TPU v7x, 32 devices: a whole 2x2x4 slice. The times are simulated.
32 devices in a mesh: dp: 8 (over z, x), ctx: 4 (over y, core).
Axes of the slice: x: 2, y: 2, z: 4, core: 2. Of those that a mesh axis runs over, the one named last changes fastest.
Arguments:
- inputs: bfloat16 [8, 512, 2048], P('dp', 'ctx'), may hold values from -8 to 8
- doc_ids: int32 [8, 512], P('dp', 'ctx'), may hold values from 0 to 3, never falling along the last dimension, each value on 1 to 256 neighbouring positions
- dilation: int32 [1], replicated, may hold values from 1 to 256
- filter_w: bfloat16 [2, 2048, 2048], P(None, 'dp', 'ctx'), may hold values from -0.09375 to 0.09375
- gate_w: bfloat16 [2, 2048, 2048], P(None, 'dp', 'ctx'), may hold values from -0.09375 to 0.09375
- filter_m: float32 [2, 2048, 2048], P(None, 'dp', 'ctx'), may hold values from -0.01171875 to 0.01171875
- filter_v: float32 [2, 2048, 2048], P(None, 'dp', 'ctx'), may hold values from 1e-07 to 4e-06
- gate_m: float32 [2, 2048, 2048], P(None, 'dp', 'ctx'), may hold values from -0.01171875 to 0.01171875
- gate_v: float32 [2, 2048, 2048], P(None, 'dp', 'ctx'), may hold values from 1e-07 to 4e-06
- cotangent: bfloat16 [8, 512, 2048], P('dp', 'ctx'), may hold values from -6 to 6
Outputs:
- layer_out: bfloat16 [8, 512, 2048], P('dp', 'ctx')
- input_grad: bfloat16 [8, 512, 2048], P('dp', 'ctx')
- new_filter_w: bfloat16 [2, 2048, 2048], P(None, 'dp', 'ctx')
- new_gate_w: bfloat16 [2, 2048, 2048], P(None, 'dp', 'ctx')
- new_filter_m: float32 [2, 2048, 2048], P(None, 'dp', 'ctx')
- new_filter_v: float32 [2, 2048, 2048], P(None, 'dp', 'ctx')
- new_gate_m: float32 [2, 2048, 2048], P(None, 'dp', 'ctx')
- new_gate_v: float32 [2, 2048, 2048], P(None, 'dp', 'ctx')
Inputs may be any that keep to these rules, and one draw needn't show every extreme that they name: `doc_ids`: document numbers never fall along a sequence; a document covers at most 256 positions.
All inputs are finite; a program needn't handle non-finite values.
Results may differ from a plain program's by a relative error of at most 0.0075.
Values may be sent and summed in bfloat16 or wider, within the bound.
No kernel may reach another device: no remote copies, remote signals or barrier semaphores. Data moves between devices by JAX's collectives and lax.ppermute only.
A program may use at most 128 MiB of HBM per device.

v0:
```python
import jax
import jax.numpy as jnp
from jax import lax
from jax.sharding import PartitionSpec as P

STEP = 10
BETA_ONE = 0.9
BETA_TWO = 0.95
LEARN_RATE = 0.001
EPSILON = 1e-08


def lagged_rows(sequence, seq_ids, shift_by):
    length = sequence.shape[0]
    start_row = length - shift_by
    padded = jnp.concatenate([jnp.zeros_like(sequence), sequence], axis=0)
    shifted = lax.dynamic_slice_in_dim(padded, start_row, length, 0)
    id_padded = jnp.concatenate([jnp.full((length,), -1, jnp.int32), seq_ids], axis=0)
    id_shifted = lax.dynamic_slice_in_dim(id_padded, start_row, length, 0)
    return jnp.where((id_shifted == seq_ids)[:, None], shifted, jnp.zeros_like(shifted))


def adam_update(weight, moment, second, gradient):
    new_moment = BETA_ONE * moment + (1.0 - BETA_ONE) * gradient
    new_second = BETA_TWO * second + (1.0 - BETA_TWO) * gradient * gradient
    first_fix = 1.0 - BETA_ONE**STEP
    second_fix = 1.0 - BETA_TWO**STEP
    step_size = new_moment / first_fix / (jnp.sqrt(new_second / second_fix) + EPSILON)
    new_weight = (weight.astype(jnp.float32) - LEARN_RATE * step_size).astype(jnp.bfloat16)
    return (new_weight, new_moment, new_second)


def per_device(
    inputs, doc_ids, dilation, filter_w, gate_w, filter_m, filter_v, gate_m, gate_v, cotangent
):
    gathered, gathered_ids = (
        lax.all_gather(inputs, "ctx", axis=1, tiled=True),
        lax.all_gather(doc_ids, "ctx", axis=1, tiled=True),
    )
    sequence = gathered[0]
    seq_ids = gathered_ids[0]
    shift_by = dilation[0]
    lagged = lagged_rows(sequence, seq_ids, shift_by)
    length = sequence.shape[0]
    columns = filter_w.shape[2]
    part_filter = lax.all_gather(filter_w, "dp", axis=1, tiled=True)
    part_gate = lax.all_gather(gate_w, "dp", axis=1, tiled=True)
    seq_cols = sequence
    lag_cols = lagged
    zero_part = jnp.concatenate([part_filter[0], part_gate[0]], axis=1)
    one_part = jnp.concatenate([part_filter[1], part_gate[1]], axis=1)
    pre_act = jnp.dot(seq_cols, zero_part, preferred_element_type=jnp.float32) + jnp.dot(
        lag_cols, one_part, preferred_element_type=jnp.float32
    )
    filter_tanh = jnp.tanh(pre_act[:, :columns])
    gate_sigmoid = jax.nn.sigmoid(pre_act[:, columns:])
    gated_cols = (filter_tanh * gate_sigmoid).astype(jnp.bfloat16)
    gated_rows = lax.all_to_all(gated_cols, "ctx", split_axis=0, concat_axis=1, tiled=True)
    layer_out = (inputs[0].astype(jnp.float32) + gated_rows.astype(jnp.float32)).astype(
        jnp.bfloat16
    )
    cot_cols = lax.all_to_all(cotangent[0], "ctx", split_axis=1, concat_axis=0, tiled=True)
    cot_float = cot_cols.astype(jnp.float32)
    filter_delta = (cot_float * gate_sigmoid * (1.0 - filter_tanh * filter_tanh)).astype(
        jnp.bfloat16
    )
    gate_delta = (cot_float * filter_tanh * gate_sigmoid * (1.0 - gate_sigmoid)).astype(
        jnp.bfloat16
    )
    pre_grad = jnp.concatenate([filter_delta, gate_delta], axis=1)
    back_filter, back_gate = (
        lax.all_gather(filter_w, "dp", axis=1, tiled=True),
        lax.all_gather(gate_w, "dp", axis=1, tiled=True),
    )
    back_zero = jnp.concatenate([back_filter[0], back_gate[0]], axis=1)
    back_one = jnp.concatenate([back_filter[1], back_gate[1]], axis=1)
    ahead_grad = jnp.concatenate([pre_grad, jnp.zeros_like(pre_grad)], axis=0)
    ahead_ids = jnp.concatenate([seq_ids, jnp.full((length,), -1, jnp.int32)], axis=0)
    row_count = cotangent.shape[1] * lax.axis_size("ctx")
    rows_ahead = lax.dynamic_slice_in_dim(ahead_grad, shift_by, row_count, 0)
    ids_later = lax.dynamic_slice_in_dim(ahead_ids, shift_by, row_count, 0)
    near_term = lax.dot_general(
        pre_grad, back_zero, (((1,), (1,)), ((), ())), preferred_element_type=jnp.float32
    )
    far_term = lax.dot_general(
        rows_ahead, back_one, (((1,), (1,)), ((), ())), preferred_element_type=jnp.float32
    )
    input_sum = lax.psum_scatter(
        (
            near_term
            + jnp.where((ids_later == seq_ids)[:, None], far_term, jnp.zeros_like(far_term))
        ).astype(jnp.bfloat16),
        "ctx",
        scatter_dimension=0,
        tiled=True,
    ).astype(jnp.float32)
    input_grad = (cotangent[0].astype(jnp.float32) + input_sum).astype(jnp.bfloat16)
    seq_cols = sequence
    lag_cols = lagged
    grad_zero = lax.dot_general(
        seq_cols, pre_grad, (((0,), (0,)), ((), ())), preferred_element_type=jnp.float32
    )
    grad_one = lax.dot_general(
        lag_cols, pre_grad, (((0,), (0,)), ((), ())), preferred_element_type=jnp.float32
    )
    summed = lax.psum_scatter(
        jnp.stack([grad_zero, grad_one], axis=1), "dp", scatter_dimension=0, tiled=True
    )
    tokens_all = length * lax.axis_size("dp")
    filter_grad = jnp.transpose(summed[:, :, :columns], (1, 0, 2)) / tokens_all
    gate_grad = jnp.transpose(summed[:, :, columns:], (1, 0, 2)) / tokens_all
    new_filter_w, new_filter_m, new_filter_v = adam_update(
        filter_w, filter_m, filter_v, filter_grad
    )
    new_gate_w, new_gate_m, new_gate_v = adam_update(gate_w, gate_m, gate_v, gate_grad)
    return (
        layer_out[None],
        input_grad[None],
        new_filter_w,
        new_gate_w,
        new_filter_m,
        new_filter_v,
        new_gate_m,
        new_gate_v,
    )


def solution(mesh):
    placed = (
        P("dp", "ctx", None),
        P("dp", "ctx"),
        P(),
        P(None, "dp", "ctx"),
        P(None, "dp", "ctx"),
        P(None, "dp", "ctx"),
        P(None, "dp", "ctx"),
        P(None, "dp", "ctx"),
        P(None, "dp", "ctx"),
        P("dp", "ctx", None),
    )
    return jax.shard_map(
        per_device,
        mesh=mesh,
        in_specs=placed,
        out_specs=(
            P("dp", "ctx", None),
            P("dp", "ctx", None),
            P(None, "dp", "ctx"),
            P(None, "dp", "ctx"),
            P(None, "dp", "ctx"),
            P(None, "dp", "ctx"),
            P(None, "dp", "ctx"),
            P(None, "dp", "ctx"),
        ),
        check_vma=False,
    )
```

profile of v0, /device:TPU:0, one launch (start us, length us, event | category | flops | bytes accessed | tf_op | source)
XLA Modules:
  0.0 541.8 jit_solution(2864115587601302465)
XLA Ops:
  9.4 1.4 all_to_all.22
  11.7 4.3 all-to-all-start.1
  16.7 9.1 %all_gather.17 = s32[1,512]{1,0:T(1,128)S(1)} all-gather(s32[1,128]{1,0:T(1,128)S(1)} %copy-done.17), channel_id=1, replica_groups=mesh['dp'=8,'ctx'=4] {'ctx'}, dimensions={1}, use_global_device_ids=true | all-gather | bytes 2560 | tf_op jit(solution)/shard_map/all_gather | solution.py:38
  25.8 59.9 %all-gather.6.cloned.1.call-done = bf16[2,2048,512]{2,1,0:T(8,128)(2,1)} async-done(((bf16[2,256,512]{2,1,0:T(8,128)(2,1)}), bf16[2,2048,512]{2,1,0:T(8,128)(2,1)}) %all-gather.6.cloned.1.call-update) | async-done | bytes 4194320 | tf_op jit(solution)/shard_map/all_gather | solution.py:47
  85.7 3.8 slice_bitcast_fusion.2
  89.5 69.7 %all-gather.4.cloned.1.call-done = bf16[2,2048,512]{2,1,0:T(8,128)(2,1)} async-done(((bf16[2,256,512]{2,1,0:T(8,128)(2,1)}), bf16[2,2048,512]{2,1,0:T(8,128)(2,1)}) %all-gather.4.cloned.1.call-update) | async-done | bytes 4194320 | tf_op jit(solution)/shard_map/all_gather | solution.py:46
  159.2 4.5 slice_bitcast_fusion.3
  163.7 18.2 %all-gather.8.cloned.1.call-done = bf16[1,512,2048]{2,1,0:T(8,128)(2,1)} async-done(((bf16[1,128,2048]{2,1,0:T(8,128)(2,1)}), bf16[1,512,2048]{2,1,0:T(8,128)(2,1)}) %all-gather.8.cloned.1.call-update) | async-done | bytes 2097168 | tf_op jit(solution)/shard_map/all_gather | solution.py:37
  181.9 4.6 fusion
  186.6 2.3 bitcast_add_fusion
  188.9 1.4 fusion.9
  191.4 2.4 fusion.1
  193.9 1.4 copy-done.7
  195.4 3.8 add_convert_fusion
  200.2 2.6 convolution_bitcast_fusion
  202.8 2.4 convolution_bitcast_fusion.1
  205.2 6.2 %pad_maximum_fusion = f32[2048,2,1024]{0,2,1:T(8,128)} fusion(f32[2048,1,1024]{0,2,1:T(8,128)S(1)} %convolution_bitcast_fusion, f32[2048,1,1024]{0,2,1:T(8,128)S(1)} %convolution_bitcast_fusion.1), kind=kLoop, calls=%fused_computation | loop fusion | flops 4194304 | bytes 33554432 | tf_op jit(solution)/shard_map/stack | solution.py:107
  211.4 4.5 all-to-all-start
  218.6 1.6 copy.23
  220.2 2.5 copy.21
  222.7 7.7 %all-to-all-done = bf16[4,128,512]{2,1,0:T(8,128)(2,1)} async-done(((bf16[4,128,512]{2,1,0:T(8,128)(2,1)}), bf16[4,128,512]{2,1,0:T(8,128)(2,1)}, u32[]{:S(2)}, u32[]{:S(2)}) %all-to-all-start) | async-done | bytes 524320 | tf_op jit(solution)/shard_map/all_to_all | solution.py:58
  231.7 1.7 copy.18
  233.3 2.9 reshape.41
  236.2 2.3 add_convert_fusion.1
  238.5 2.1 fusion.13
  240.6 279.5 %reduce-scatter.5.cloned.1.call-done = f32[256,2,1024]{0,2,1:T(8,128)} async-done(((f32[2048,2,1024]{0,2,1:T(8,128)}), f32[256,2,1024]{0,2,1:T(8,128)}) %reduce-scatter.5.cloned.1.call-update) | async-done | bytes 2097168 | tf_op jit(solution)/shard_map/reduce_scatter | solution.py:106
  520.1 5.7 %subtract_convert_fusion = (bf16[2,256,512]{1,2,0:T(8,128)(2,1)}, f32[2,256,512]{1,2,0:T(8,128)}, f32[2,256,512]{1,2,0:T(8,128)}, bf16[2,256,512]{1,2,0:T(8,128)...) fusion(bf16[2,256,512]{1,2,0:T(8,128)(2,1)} %copy.24, f32[256,2,1024]{0,2,1:T(8,128)} %reduce-scatter.5.cloned.1.call-done, ...), kind=kLoop, calls=%fused_computation.37 | loop fusion | flops 8388608 | bytes 12582912 | tf_op jit(solution)/shard_map/convert_element_type | solution.py:29
  525.8 2.2 copy.27
  528.0 2.0 copy.28
  530.0 1.3 copy.29
  531.3 1.3 copy.30
  533.9 1.3 copy.32
  (60 shorter events, 10.6 us)
Async XLA Ops:
  7.2 78.5 %all-gather.6.cloned.1.call-start = ((), (), s32[]{:S(2)}) async-start(), calls=%async_computation.5 | async-start | bytes 4718592 | tf_op jit(solution)/shard_map/all_gather | solution.py:47
  7.9 8.7 %copy-start.17 = (s32[1,128]{1,0:T(1,128)S(1)}, s32[1,128]{1,0:T(1,128)}, u32[]{:S(2)}) copy-start(s32[1,128]{1,0:T(1,128)} %param.11) | copy-start | bytes 1540
  7.9 151.3 %all-gather.4.cloned.1.call-start = ((), (), s32[]{:S(2)}) async-start(), calls=%async_computation.4 | async-start | bytes 4718592 | tf_op jit(solution)/shard_map/all_gather | solution.py:46
  8.7 173.3 %all-gather.8.cloned.1.call-start = ((), (), s32[]{:S(2)}) async-start(), calls=%async_computation.6 | async-start | bytes 2621440 | tf_op jit(solution)/shard_map/all_gather | solution.py:37
  11.7 177.2 %all-to-all-start.1 = ((bf16[128,4,512]{2,0,1:T(8,128)(2,1)}), bf16[128,4,512]{2,0,1:T(8,128)(2,1)S(1)}, u32[]{:S(2)}, u32[]{:S(2)}) async-start(bf16[128,4,512]{2,0,1:T(8,128)(2,1)} %copy.19), calls=%async_computation.1 | async-start | bytes 1048576 | tf_op jit(solution)/shard_map/all_to_all | solution.py:62
  16.0 222.5 %reduce-scatter.3.cloned.1.call-start = ((), (), s32[]{:S(2)}) async-start(), calls=%async_computation.7 | async-start | bytes 2621440 | tf_op jit(solution)/shard_map/reduce_scatter | solution.py:88
  89.5 92.4 %copy-start.6 = (bf16[2048,512]{1,0:T(8,128)(2,1)}, bf16[2048,512]{1,0:T(8,128)(2,1)S(1)}, u32[]{:S(2)}) copy-start(bf16[2048,512]{1,0:T(8,128)(2,1)S(1)} %get-tuple-element.25) | copy-start | bytes 6291460
  181.9 4.6 copy-start.8
  181.9 4.6 copy-start.11
  181.9 4.6 copy-start.18
  188.9 1.6 copy-start.9
  188.9 2.5 copy-start.12
  190.3 3.4 copy-start.13
  191.4 2.5 copy-start.10
  193.8 1.6 copy-start.7
  195.4 4.1 copy-start.19
  199.2 1.0 copy-start.14
  199.2 320.9 %reduce-scatter.5.cloned.1.call-start = ((), (), s32[]{:S(2)}) async-start(), calls=%async_computation.8 | async-start | bytes 18874368 | tf_op jit(solution)/shard_map/reduce_scatter | solution.py:106
  211.4 4.6 copy-start.4
  211.4 5.6 %copy-start.5 = (bf16[2,256,512]{2,1,0:T(8,128)(2,1)S(1)}, bf16[2,256,512]{2,1,0:T(8,128)(2,1)}, u32[]{:S(2)}) copy-start(bf16[2,256,512]{2,1,0:T(8,128)(2,1)} %param.13) | copy-start | bytes 1572868
  211.4 6.6 %copy-start.15 = (f32[2,256,512]{2,1,0:T(8,128)S(1)}, f32[2,256,512]{2,1,0:T(8,128)}, u32[]{:S(2)}) copy-start(f32[2,256,512]{2,1,0:T(8,128)} %param.17) | copy-start | bytes 3145732
  211.4 19.1 %all-to-all-start = ((bf16[4,128,512]{2,1,0:T(8,128)(2,1)}), bf16[4,128,512]{2,1,0:T(8,128)(2,1)}, u32[]{:S(2)}, u32[]{:S(2)}) async-start(bf16[4,128,512]{2,1,0:T(8,128)(2,1)} %bitcast.8), calls=%async_computation | async-start | bytes 1048576 | tf_op jit(solution)/shard_map/all_to_all | solution.py:58
  215.9 2.4 copy-start.16
  525.8 4.2 copy-start.3
  525.8 5.6 %copy-start.2 = (f32[2,256,512]{1,2,0:T(8,128)S(1)}, f32[2,256,512]{1,2,0:T(8,128)}, u32[]{:S(2)}) copy-start(f32[2,256,512]{1,2,0:T(8,128)} %get-tuple-element.29) | copy-start | bytes 3145732
  530.0 2.6 copy-start.1
  531.3 2.6 copy-start
Sparse Core Ops, SparseCore 0:
  10.2 75.4 all-gather.5
  87.9 71.2 all-gather.3
  160.8 21.0 all-gather.7
  199.3 36.7 reduce-scatter.2
  239.8 280.2 reduce-scatter.4
where the time goes:
time: 542 us
  waiting for transfers between devices  437 us (81%)
  local copies, waits for them, and re-layouts  34.8 us (6%)
  other arithmetic  19 us (4%)
  matrix products  18.1 us (3%)
  between operations  14.7 us (3%)
  starting transfers between devices  9.11 us (2%)
  blocking collectives  9.06 us (2%)
    reduce_scatter x1, waiting for transfers between devices, per_device(): lax.psum_scatter(jnp.stack([grad_zero, grad_one], axis=1), 'dp', scatter_...  279 us
    all_gather x1, waiting for transfers between devices, per_device(): part_filter = lax.all_gather(filter_w, 'dp', axis=1, tiled=True)  69.7 us
    all_gather x1, waiting for transfers between devices, per_device(): part_gate = lax.all_gather(gate_w, 'dp', axis=1, tiled=True)  59.9 us
    unnamed x52, local copies, waits for them, and re-layouts  19.5 us
    all_gather x1, waiting for transfers between devices, per_device(): lax.all_gather(inputs, 'ctx', axis=1, tiled=True)  18.2 us
  transfers between devices with their start and end apart: 7, of which 5 were waited for; matrix products, arithmetic and copies ran while one was open for 8% of the time, Pallas kernels for 0%

commit v1 on v0

--- a/solution.py
+++ b/solution.py
@@ -2,12 +2,20 @@
 import jax.numpy as jnp
 from jax import lax
 from jax.sharding import PartitionSpec as P
+from jax.lax import axis_index, axis_size, ppermute
 
 STEP = 10
 BETA_ONE = 0.9
 BETA_TWO = 0.95
 LEARN_RATE = 0.001
 EPSILON = 1e-08
+
+
+def edit_ranges(w_in, d0):
+    reached = list(w_in.shape[1:])
+    reached[d0] *= w_in.shape[0]
+    mid_arr = jnp.moveaxis(w_in, 0, d0).reshape(reached)
+    return mid_arr
 
 
 def lagged_rows(sequence, seq_ids, shift_by):
@@ -44,7 +52,22 @@
     length = sequence.shape[0]
     columns = filter_w.shape[2]
     part_filter = lax.all_gather(filter_w, "dp", axis=1, tiled=True)
-    part_gate = lax.all_gather(gate_w, "dp", axis=1, tiled=True)
+    slots = axis_size("dp")
+    store = tuple(((k0, (k0 + 1) % slots) for k0 in range(slots)))
+    sides = tuple(((w, ix) for ix, w in store))
+    near, top = ([], [])
+    for dev_i in range(slots - 1):
+        if dev_i % 2 == 0:
+            out_arr = ppermute(near[-1] if near else gate_w, axis_name="dp", perm=store)
+            near.append(out_arr)
+        else:
+            later = ppermute(top[-1] if top else gate_w, axis_name="dp", perm=sides)
+            top.append(later)
+    fresh = jnp.stack([*near[::-1], gate_w, *top], axis=0)
+    w_next = axis_index("dp")
+    extra = w_next - len(near)
+    fresh = fresh[(jnp.arange(slots) - extra) % slots]
+    part_gate = edit_ranges(fresh, 1)
     seq_cols = sequence
     lag_cols = lagged
     zero_part = jnp.concatenate([part_filter[0], part_gate[0]], axis=1)

time: 542 us -> 585 us (1.079)
  local copies, waits for them, and re-layouts: 34.8 us -> 51.1 us
  starting transfers between devices: 9.11 us -> 25.4 us
  waiting for transfers between devices: 437 us -> 445 us
    ppermute x0 -> x7, waiting for transfers between devices: none -> 72.9 us  [the longest x4 71.9 us: per_device(): out_arr = ppermute(near[-1] if near else gate_w, axis_name='dp', perm=store)]
    all_gather x1, waiting for transfers between devices: 69.7 us -> 0.88 us  [per_device(): part_filter = lax.all_gather(filter_w, 'dp', axis=1, tiled=True)]
    ppermute x0 -> x7, starting transfers between devices: none -> 17.2 us  [the longest x3 11.2 us: per_device(): later = ppermute(top[-1] if top else gate_w, axis_name='dp', perm=sides)]
    unnamed x52 -> x61, local copies, waits for them, and re-layouts: 19.5 us -> 27.5 us
  transfers between devices with their start and end apart: 7 -> 14, of which waited for: 5 -> 10; matrix products, arithmetic and copies ran while one was open for 8% -> 11% of each run, Pallas kernels for 0% -> 0%
where the time goes in v1:
time: 585 us
  waiting for transfers between devices  445 us (76%)
  local copies, waits for them, and re-layouts  51.1 us (9%)
  starting transfers between devices  25.4 us (4%)
  other arithmetic  19.9 us (3%)
  matrix products  19.7 us (3%)
  between operations  14.7 us (3%)
  blocking collectives  8.98 us (2%)
    reduce_scatter x1, waiting for transfers between devices, per_device(): lax.psum_scatter(jnp.stack([grad_zero, grad_one], axis=1), 'dp', scatter_...  277 us
    ppermute x4, waiting for transfers between devices, per_device(): out_arr = ppermute(near[-1] if near else gate_w, axis_name='dp', perm=store)  71.9 us
    all_gather x1, waiting for transfers between devices, per_device(): lax.all_gather(gate_w, 'dp', axis=1, tiled=True)  64.6 us
    unnamed x61, local copies, waits for them, and re-layouts  27.5 us
    all_gather x1, waiting for transfers between devices, per_device(): lax.all_gather(inputs, 'ctx', axis=1, tiled=True)  19.2 us
  transfers between devices with their start and end apart: 14, of which 10 were waited for; matrix products, arithmetic and copies ran while one was open for 11% of the time, Pallas kernels for 0%

profile of v1, /device:TPU:0, one launch (start us, length us, event | category | flops | bytes accessed | tf_op | source)
XLA Modules:
  0.0 584.6 jit_solution(14832088534337028818)
XLA Ops:
  9.4 3.0 collective-permute-start
  12.4 16.8 %collective-permute-done = bf16[2,256,512]{2,1,0:T(8,128)(2,1)S(1)} collective-permute-done((bf16[2,256,512]{2,1,0:T(8,128)(2,1)}, bf16[2,256,512]{2,1,0:T(8,128)(2,1)S(1)}, u32[]{:S(2)}, u32[]{:S(2)}) %collective-permute-start) | collective-permute-done | bytes 524320 | tf_op jit(solution)/shard_map/ppermute | solution.py:61
  29.7 4.3 collective-permute-start.4
  34.0 21.8 %collective-permute-done.1 = bf16[2,256,512]{2,1,0:T(8,128)(2,1)S(1)} collective-permute-done((bf16[2,256,512]{2,1,0:T(8,128)(2,1)S(1)}, bf16[2,256,512]{2,1,0:T(8,128)(2,1)S(1)}, u32[]{:S(2)}, u32[]{:S(2)}) %collective-permute-start.1) | collective-permute-done | bytes 524320 | tf_op jit(solution)/shard_map/ppermute | solution.py:61
  55.8 4.7 collective-permute-start.5
  60.5 27.2 %collective-permute-done.2 = bf16[2,256,512]{2,1,0:T(8,128)(2,1)} collective-permute-done((bf16[2,256,512]{2,1,0:T(8,128)(2,1)S(1)}, bf16[2,256,512]{2,1,0:T(8,128)(2,1)}, u32[]{:S(2)}, u32[]{:S(2)}) %collective-permute-start.2) | collective-permute-done | bytes 524320 | tf_op jit(solution)/shard_map/ppermute | solution.py:61
  87.7 2.6 collective-permute-start.3
  92.6 3.5 all-to-all-start.1
  96.8 9.0 %all_gather.15 = s32[1,512]{1,0:T(1,128)S(1)} all-gather(s32[1,128]{1,0:T(1,128)S(1)} %copy-done.18), channel_id=1, replica_groups=mesh['dp'=8,'ctx'=4] {'ctx'}, dimensions={1}, use_global_device_ids=true | all-gather | bytes 2560 | tf_op jit(solution)/shard_map/all_gather | solution.py:46
  108.0 6.1 %collective-permute-done.3 = bf16[2,256,512]{2,1,0:T(8,128)(2,1)} collective-permute-done((bf16[2,256,512]{2,1,0:T(8,128)(2,1)}, bf16[2,256,512]{2,1,0:T(8,128)(2,1)}, u32[]{:S(2)}, u32[]{:S(2)}) %collective-permute-start.3) | collective-permute-done | bytes 524320 | tf_op jit(solution)/shard_map/ppermute | solution.py:61
  125.0 4.9 gather_fusion
  129.9 4.6 fusion.37
  135.3 3.8 slice_bitcast_fusion.3
  139.2 19.2 %all-gather.6.cloned.1.call-done = bf16[1,512,2048]{2,1,0:T(8,128)(2,1)} async-done(((bf16[1,128,2048]{2,1,0:T(8,128)(2,1)}), bf16[1,512,2048]{2,1,0:T(8,128)(2,1)}) %all-gather.6.cloned.1.call-update) | async-done | bytes 2097168 | tf_op jit(solution)/shard_map/all_gather | solution.py:45
  158.3 4.6 fusion
  163.0 2.3 bitcast_add_fusion
  168.8 64.6 %all-gather.8.cloned.1.call-done = bf16[2,2048,512]{2,1,0:T(8,128)(2,1)} async-done(((bf16[2,256,512]{2,1,0:T(8,128)(2,1)}), bf16[2,2048,512]{2,1,0:T(8,128)(2,1)}) %all-gather.8.cloned.1.call-update) | async-done | bytes 4194320 | tf_op jit(solution)/shard_map/all_gather | solution.py:96
  233.3 2.6 slice_bitcast_fusion.1
  236.0 2.5 fusion.1
  238.5 3.8 add_convert_fusion
  242.6 4.1 convolution_bitcast_fusion
  246.7 2.4 convolution_bitcast_fusion.1
  249.1 6.1 %pad_maximum_fusion = f32[2048,2,1024]{0,2,1:T(8,128)} fusion(f32[2048,1,1024]{0,2,1:T(8,128)S(1)} %convolution_bitcast_fusion, f32[2048,1,1024]{0,2,1:T(8,128)S(1)} %convolution_bitcast_fusion.1), kind=kLoop, calls=%fused_computation.1 | loop fusion | flops 4194304 | bytes 33554432 | tf_op jit(solution)/shard_map/stack | solution.py:130
  255.2 4.3 all-to-all-start
  263.8 2.5 copy.21
  266.3 8.1 %all-to-all-done = bf16[4,128,512]{2,1,0:T(8,128)(2,1)} async-done(((bf16[4,128,512]{2,1,0:T(8,128)(2,1)}), bf16[4,128,512]{2,1,0:T(8,128)(2,1)}, u32[]{:S(2)}, u32[]{:S(2)}) %all-to-all-start) | async-done | bytes 524320 | tf_op jit(solution)/shard_map/all_to_all | solution.py:81
  277.3 2.9 reshape.95
  280.2 2.3 add_convert_fusion.1
  284.6 277.1 %reduce-scatter.5.cloned.1.call-done = f32[256,2,1024]{0,2,1:T(8,128)} async-done(((f32[2048,2,1024]{0,2,1:T(8,128)}), f32[256,2,1024]{0,2,1:T(8,128)}) %reduce-scatter.5.cloned.1.call-update) | async-done | bytes 2097168 | tf_op jit(solution)/shard_map/reduce_scatter | solution.py:129
  561.7 5.7 subtract_convert_fusion
  567.4 2.2 copy.27
  571.6 2.5 copy.29
  (88 shorter events, 37.9 us)
Async XLA Ops:
  7.2 89.6 %copy-start.18 = (s32[1,128]{1,0:T(1,128)S(1)}, s32[1,128]{1,0:T(1,128)}, u32[]{:S(2)}) copy-start(s32[1,128]{1,0:T(1,128)} %param.11) | copy-start | bytes 1540
  7.2 128.2 %all-gather.4.cloned.1.call-start = ((), (), s32[]{:S(2)}) async-start(), calls=%async_computation.4 | async-start | bytes 4718592 | tf_op jit(solution)/shard_map/all_gather | solution.py:54
  7.9 111.7 %copy-start = (bf16[2,256,512]{2,1,0:T(8,128)(2,1)S(1)}, bf16[2,256,512]{2,1,0:T(8,128)(2,1)}, u32[]{:S(2)}) copy-start(bf16[2,256,512]{2,1,0:T(8,128)(2,1)} %param.14) | copy-start | bytes 1572868
  7.9 150.4 %all-gather.6.cloned.1.call-start = ((), (), s32[]{:S(2)}) async-start(), calls=%async_computation.5 | async-start | bytes 2621440 | tf_op jit(solution)/shard_map/all_gather | solution.py:45
  8.7 224.7 %all-gather.8.cloned.1.call-start = ((), (), s32[]{:S(2)}) async-start(), calls=%async_computation.6 | async-start | bytes 4718592 | tf_op jit(solution)/shard_map/all_gather | solution.py:96
  9.4 19.9 %collective-permute-start = (bf16[2,256,512]{2,1,0:T(8,128)(2,1)}, bf16[2,256,512]{2,1,0:T(8,128)(2,1)S(1)}, u32[]{:S(2)}, u32[]{:S(2)}) collective-permute-start(bf16[2,256,512]{2,1,0:T(8,128)(2,1)} %param.14), channel_id=1, source_target_pairs={{0,4},{4,8},{8,12},{12,16},{16,20},{20,24},{24,28},{28,0},{1,5},{5... | collective-permute-start | bytes 1572872 | tf_op jit(solution)/shard_map/ppermute | solution.py:61
  29.3 26.5 %collective-permute-start.1 = (bf16[2,256,512]{2,1,0:T(8,128)(2,1)S(1)}, bf16[2,256,512]{2,1,0:T(8,128)(2,1)S(1)}, u32[]{:S(2)}, u32[]{:S(2)}) collective-permute-start(bf16[2,256,512]{2,1,0:T(8,128)(2,1)S(1)} %collective-permute-done), channel_id=1, source_target_pairs={{0,4},{4,8},{8,12},{12,16},{16,20},{20,24},{24,28},{28,0},{1,5},{5... | collective-permute-start | bytes 1572872 | tf_op jit(solution)/shard_map/ppermute | solution.py:61
  29.7 26.1 %collective-permute-start.4 = (bf16[2,256,512]{2,1,0:T(8,128)(2,1)}, bf16[2,256,512]{2,1,0:T(8,128)(2,1)S(1)}, u32[]{:S(2)}, u32[]{:S(2)}) collective-permute-start(bf16[2,256,512]{2,1,0:T(8,128)(2,1)} %param.14), channel_id=1, source_target_pairs={{4,0},{8,4},{12,8},{16,12},{20,16},{24,20},{28,24},{0,28},{5,1},{9... | collective-permute-start | bytes 1572872 | tf_op jit(solution)/shard_map/ppermute | solution.py:64
  55.8 31.9 %collective-permute-start.2 = (bf16[2,256,512]{2,1,0:T(8,128)(2,1)S(1)}, bf16[2,256,512]{2,1,0:T(8,128)(2,1)}, u32[]{:S(2)}, u32[]{:S(2)}) collective-permute-start(bf16[2,256,512]{2,1,0:T(8,128)(2,1)S(1)} %collective-permute-done.1), channel_id=1, source_target_pairs={{0,4},{4,8},{8,12},{12,16},{16,20},{20,24},{24,28},{28,0},{1,5},{5... | collective-permute-start | bytes 1572872 | tf_op jit(solution)/shard_map/ppermute | solution.py:61
  55.8 50.1 %collective-permute-start.5 = (bf16[2,256,512]{2,1,0:T(8,128)(2,1)S(1)}, bf16[2,256,512]{2,1,0:T(8,128)(2,1)}, u32[]{:S(2)}, u32[]{:S(2)}) collective-permute-start(bf16[2,256,512]{2,1,0:T(8,128)(2,1)S(1)} %collective-permute-done.4), channel_id=1, source_target_pairs={{4,0},{8,4},{12,8},{16,12},{20,16},{24,20},{28,24},{0,28},{5,1},{9... | collective-permute-start | bytes 1572872 | tf_op jit(solution)/shard_map/ppermute | solution.py:64
  87.7 26.5 %collective-permute-start.3 = (bf16[2,256,512]{2,1,0:T(8,128)(2,1)}, bf16[2,256,512]{2,1,0:T(8,128)(2,1)}, u32[]{:S(2)}, u32[]{:S(2)}) collective-permute-start(bf16[2,256,512]{2,1,0:T(8,128)(2,1)} %collective-permute-done.2), channel_id=1, source_target_pairs={{0,4},{4,8},{8,12},{12,16},{16,20},{20,24},{24,28},{28,0},{1,5},{5... | collective-permute-start | bytes 1572872 | tf_op jit(solution)/shard_map/ppermute | solution.py:61
  92.6 72.7 %all-to-all-start.1 = ((bf16[128,4,512]{2,0,1:T(8,128)(2,1)}), bf16[128,4,512]{2,0,1:T(8,128)(2,1)S(1)}, u32[]{:S(2)}, u32[]{:S(2)}) async-start(bf16[128,4,512]{2,0,1:T(8,128)(2,1)} %copy.19), calls=%async_computation.1 | async-start | bytes 1048576 | tf_op jit(solution)/shard_map/all_to_all | solution.py:85
  96.0 186.4 %reduce-scatter.3.cloned.1.call-start = ((), (), s32[]{:S(2)}) async-start(), calls=%async_computation.7 | async-start | bytes 2621440 | tf_op jit(solution)/shard_map/reduce_scatter | solution.py:111
  105.9 18.2 %collective-permute-start.6 = (bf16[2,256,512]{2,1,0:T(8,128)(2,1)}, bf16[2,256,512]{2,1,0:T(8,128)(2,1)S(1)}, u32[]{:S(2)}, u32[]{:S(2)}) collective-permute-start(bf16[2,256,512]{2,1,0:T(8,128)(2,1)} %collective-permute-done.5), channel_id=1, source_target_pairs={{4,0},{8,4},{12,8},{16,12},{20,16},{24,20},{28,24},{0,28},{5,1},{9... | collective-permute-start | bytes 1572872 | tf_op jit(solution)/shard_map/ppermute | solution.py:64
  139.2 23.8 %copy-start.7 = (bf16[2048,512]{1,0:T(8,128)(2,1)}, bf16[2048,512]{1,0:T(8,128)(2,1)S(1)}, u32[]{:S(2)}) copy-start(bf16[2048,512]{1,0:T(8,128)(2,1)S(1)} %get-tuple-element.27) | copy-start | bytes 6291460
  158.3 4.6 copy-start.5
  158.3 4.6 copy-start.9
  158.3 4.6 copy-start.19
  168.8 67.1 %copy-start.8 = (bf16[2048,512]{1,0:T(8,128)(2,1)S(1)}, bf16[2048,512]{1,0:T(8,128)(2,1)}, u32[]{:S(2)}) copy-start(bf16[2048,512]{1,0:T(8,128)(2,1)} %copy-done.7) | copy-start | bytes 6291460
  233.3 2.6 copy-start.17
  235.9 2.5 copy-start.6
  235.9 2.5 copy-start.11
  238.5 4.0 copy-start.14
  242.3 319.4 %reduce-scatter.5.cloned.1.call-start = ((), (), s32[]{:S(2)}) async-start(), calls=%async_computation.8 | async-start | bytes 18874368 | tf_op jit(solution)/shard_map/reduce_scatter | solution.py:129
  242.5 4.1 copy-start.20
  255.1 5.4 copy-start.4
  255.1 6.4 %copy-start.15 = (f32[2,256,512]{2,1,0:T(8,128)S(1)}, f32[2,256,512]{2,1,0:T(8,128)}, u32[]{:S(2)}) copy-start(f32[2,256,512]{2,1,0:T(8,128)} %param.17) | copy-start | bytes 3145732
  255.2 6.7 %copy-start.16 = (f32[2,256,512]{2,1,0:T(8,128)S(1)}, f32[2,256,512]{2,1,0:T(8,128)}, u32[]{:S(2)}) copy-start(f32[2,256,512]{2,1,0:T(8,128)} %param.18) | copy-start | bytes 3145732
  255.2 19.3 %all-to-all-start = ((bf16[4,128,512]{2,1,0:T(8,128)(2,1)}), bf16[4,128,512]{2,1,0:T(8,128)(2,1)}, u32[]{:S(2)}, u32[]{:S(2)}) async-start(bf16[4,128,512]{2,1,0:T(8,128)(2,1)} %bitcast.18), calls=%async_computation | async-start | bytes 1048576 | tf_op jit(solution)/shard_map/all_to_all | solution.py:81
  567.3 6.8 %copy-start.3 = (f32[2,256,512]{1,2,0:T(8,128)S(1)}, f32[2,256,512]{1,2,0:T(8,128)}, u32[]{:S(2)}) copy-start(f32[2,256,512]{1,2,0:T(8,128)} %get-tuple-element.31) | copy-start | bytes 3145732
  567.3 8.1 %copy-start.2 = (f32[2,256,512]{1,2,0:T(8,128)S(1)}, f32[2,256,512]{1,2,0:T(8,128)}, u32[]{:S(2)}) copy-start(f32[2,256,512]{1,2,0:T(8,128)} %get-tuple-element.17) | copy-start | bytes 3145732
  567.3 9.4 %copy-start.1 = (f32[2,256,512]{1,2,0:T(8,128)S(1)}, f32[2,256,512]{1,2,0:T(8,128)}, u32[]{:S(2)}) copy-start(f32[2,256,512]{1,2,0:T(8,128)} %get-tuple-element.18) | copy-start | bytes 3145732
  (3 other events, 4.3 us)
Sparse Core Ops, SparseCore 0:
  10.2 125.1 all-gather.3
  136.9 21.3 all-gather.5
  160.5 72.7 all-gather.7
  242.4 35.3 reduce-scatter.2
  281.4 280.2 reduce-scatter.4
